TPU v7x, 256 devices: a whole 4x4x8 slice. The times are simulated.
256 devices in a mesh: shard: 8 (over z_lo, x), tensor: 4 (over z_hi), section: 8 (over y, core).
Axes of the slice: x: 4, y: 4, z: 8 (z_hi: 4, z_lo: 2; z = z_hi * 2 + z_lo), core: 2. Of those that a mesh axis runs over, the one named last changes fastest.
Arguments:
- activations: bfloat16 [8, 2048, 2304], P(None, 'shard', ('tensor', 'section')), may hold values from -6 to 6
- router_grad: bfloat16 [8, 2048], P(None, 'shard'), may hold values from -6 to 6
- token_ids: int32 [2048], P('shard'), may hold values from 0 to 8191
- norm_terms: bfloat16 [2, 2048, 2304], P(None, 'shard', ('tensor', 'section'))
- old_factors: float32 [8, 2304, 2304], P('shard', 'tensor', 'section'), as said below
- old_router_factor: float32 [8, 8], replicated, as said below
- old_norm_diag: float32 [2, 2304], P(None, ('tensor', 'section')), may hold values from 0.5 to 5
- old_embed_diag: float32 [8192], P('tensor'), may hold values from 0.05 to 0.5
Outputs:
- precond_attn: float32 [4, 2304, 2304], P(None, 'tensor', 'section')
- precond_router: float32 [8, 2304], P(None, 'tensor')
- precond_norms: float32 [2, 2304], P(None, ('tensor', 'section'))
- precond_embed: float32 [8192, 2304], P('tensor', 'section')
Inputs may be any that keep to these rules, and one draw needn't show every extreme that they name: `old_factors`: each matrix is symmetric with a positive diagonal. `old_router_factor`: symmetric with a positive diagonal.
All inputs are finite; a program needn't handle non-finite values.
Results may differ from a plain program's by a relative error of at most 0.0083.
Values may be sent and summed in bfloat16 or wider, within the bound.
A program may use at most 64 MiB of HBM per device.

v0:
```python
import math
import jax
import jax.numpy as jnp
from jax import lax
from jax.sharding import PartitionSpec as P

D = 2304
EXPERTS = 8
VOCAB = 8192
factor_decay = 0.5
damping = 0.01
learning_rate = 0.05


def local_inverse(matrix):
    width = matrix.shape[0]
    trace = jnp.sum(jnp.diagonal(matrix))
    factor_scale = width / (3.0 * trace)
    identity = jnp.eye(width, dtype=jnp.float32)
    matrix_low = lax.optimization_barrier(matrix.astype(jnp.bfloat16))
    first = 2.0 * factor_scale * identity - factor_scale * factor_scale * matrix_low.astype(
        jnp.float32
    )
    first_low = first.astype(jnp.bfloat16)
    image = jnp.dot(matrix_low, first_low, preferred_element_type=jnp.float32).astype(jnp.bfloat16)
    product = jnp.dot(first_low, image, preferred_element_type=jnp.float32)
    return (2.0 * first - product).astype(jnp.bfloat16)


def fold_with(columns, piece):
    return jnp.einsum("kij,kjl->kil", piece, columns, preferred_element_type=jnp.float32)


def per_device(
    activations,
    router_grad,
    token_ids,
    norm_terms,
    old_factors,
    old_router_factor,
    old_norm_diag,
    old_embed_diag,
):
    n_tensor = lax.axis_size("tensor")
    n_section = lax.axis_size("section")
    n_shard = lax.axis_size("shard")
    tensor_rank = lax.axis_index("tensor")
    section_rank = lax.axis_index("section")
    row_block = D // n_tensor
    col_block = D // n_section
    tokens_all = activations.shape[1] * n_shard
    row_start = tensor_rank * row_block
    col_start = section_rank * col_block

    def collect(carry, piece):
        whole = lax.all_gather(piece, ("tensor", "section"), axis=1, tiled=True)
        rows_part = lax.dynamic_slice_in_dim(whole, row_start, row_block, 1)
        cols_part = lax.dynamic_slice_in_dim(whole, col_start, col_block, 1)
        return (carry, (rows_part, cols_part))

    unused_carry, (row_parts, col_parts) = lax.scan(collect, jnp.int32(0), activations)
    partial_value = jnp.einsum(
        "mnr,mnc->mrc", row_parts, col_parts, preferred_element_type=jnp.float32
    )
    fresh = lax.psum_scatter(partial_value, "shard", scatter_dimension=0, tiled=True) / tokens_all
    row_index = lax.broadcasted_iota(jnp.int32, (row_block, col_block), 0) + row_start
    col_index = lax.broadcasted_iota(jnp.int32, (row_block, col_block), 1) + col_start
    eye_block = (row_index == col_index).astype(jnp.float32)
    matrix = factor_decay * old_factors + (1.0 - factor_decay) * fresh + damping * eye_block
    diag_part = jnp.sum(matrix * eye_block, axis=(1, 2))
    trace = lax.psum(diag_part, ("tensor", "section"))
    factor_scale = (D / (3.0 * trace))[:, None, None]
    matrix_low = lax.optimization_barrier(matrix.astype(jnp.bfloat16))
    first = 2.0 * factor_scale * eye_block - factor_scale * factor_scale * matrix_low.astype(
        jnp.float32
    )
    first_low = first.astype(jnp.bfloat16)
    first_cols = lax.all_gather(first_low, "tensor", axis=1, tiled=True)
    image = fold_with(first_cols, lax.all_gather(matrix_low, "section", axis=2, tiled=True))
    image_cols = lax.all_gather(image.astype(jnp.bfloat16), "tensor", axis=1, tiled=True)
    product = fold_with(image_cols, lax.all_gather(first_low, "section", axis=2, tiled=True))
    inverse_low = (2.0 * first - product).astype(jnp.bfloat16)
    inverses = lax.all_gather(inverse_low, "shard", axis=0, tiled=True)
    left_terms = jnp.stack(
        [
            jnp.einsum("nc,rc->nr", col_parts[m], inverses[m], preferred_element_type=jnp.float32)
            for m in (0, 4, 6)
        ]
    )
    left = lax.psum(left_terms, "section").astype(jnp.bfloat16)
    right_terms = jnp.stack(
        [
            jnp.einsum("nr,rc->nc", row_parts[m], inverses[m], preferred_element_type=jnp.float32)
            for m in (1, 2, 3, 5, 7)
        ]
    )
    right = lax.psum(right_terms, "tensor").astype(jnp.bfloat16)
    norm_values = norm_terms.astype(jnp.float32)
    router_part = jnp.einsum(
        "en,fn->ef", router_grad, router_grad, preferred_element_type=jnp.float32
    )
    router_sum, norm_total, norm_squares = lax.psum(
        (router_part, jnp.sum(norm_values, axis=1), jnp.sum(norm_values * norm_values, axis=1)),
        "shard",
    )
    router_matrix = (
        factor_decay * old_router_factor
        + (1.0 - factor_decay) * (router_sum / tokens_all)
        + damping * jnp.eye(EXPERTS, dtype=jnp.float32)
    )
    router_inverse = local_inverse(router_matrix)
    router_right = jnp.einsum(
        "en,ef->nf", router_grad, router_inverse, preferred_element_type=jnp.float32
    ).astype(jnp.bfloat16)
    precond_norms = (
        learning_rate
        * norm_total
        / (
            factor_decay * old_norm_diag
            + (1.0 - factor_decay) * (norm_squares / tokens_all)
            + damping
        )
    )
    ids_all = lax.all_gather(token_ids, "shard", axis=0, tiled=True)
    embed_all = lax.all_gather(right[4], "shard", axis=0, tiled=True)
    paired_left = jnp.stack([left[0], left[0], left[0], left[1]])
    attn_terms = jnp.einsum(
        "wnr,wnc->wrc", paired_left, right[:4], preferred_element_type=jnp.float32
    )
    router_term = jnp.einsum("nf,nr->fr", router_right, left[2], preferred_element_type=jnp.float32)
    attn_sum, router_total = lax.psum((attn_terms, router_term), "shard")
    precond_attn = learning_rate * attn_sum
    precond_router = learning_rate * router_total
    vocab_block = VOCAB // n_tensor
    step_rows = math.gcd(vocab_block, 512)
    vocab_start = tensor_rank * vocab_block

    def embed_block(block_index):
        ids_here = vocab_start + block_index * step_rows + lax.iota(jnp.int32, step_rows)
        onehot = (ids_here[:, None] == ids_all[None, :]).astype(jnp.bfloat16)
        summed = jnp.dot(onehot, embed_all, preferred_element_type=jnp.float32)
        tallies = jnp.sum(onehot, axis=1, dtype=jnp.float32)
        return (summed, tallies)

    block_sums, block_counts = lax.map(
        embed_block, jnp.arange(vocab_block // step_rows, dtype=jnp.int32)
    )
    embed_sum = block_sums.reshape(vocab_block, col_block)
    counts = block_counts.reshape(vocab_block)
    divisor = factor_decay * old_embed_diag + (1.0 - factor_decay) * (counts / tokens_all) + damping
    precond_embed = learning_rate * embed_sum / divisor[:, None]
    return (precond_attn, precond_router, precond_norms, precond_embed)


def solution(mesh):
    return jax.shard_map(
        per_device,
        mesh=mesh,
        in_specs=(
            P(None, "shard", ("tensor", "section")),
            P(None, "shard"),
            P("shard"),
            P(None, "shard", ("tensor", "section")),
            P("shard", "tensor", "section"),
            P(),
            P(None, ("tensor", "section")),
            P("tensor"),
        ),
        out_specs=(
            P(None, "tensor", "section"),
            P(None, "tensor"),
            P(None, ("tensor", "section")),
            P("tensor", "section"),
        ),
        check_vma=False,
    )
```

profile of v0, /device:TPU:8, one launch (start us, length us, event | category | flops | bytes accessed | tf_op | source)
XLA Modules:
  0.0 1097.6 jit_solution(1544421095464947552)
XLA Ops:
  8.0 450.4 %while.26 = (s32[]{:T(128)}, bf16[8,256,576]{1,2,0:T(8,128)(2,1)S(1)}, bf16[8,256,288]{1,2,0:T(8,128)(2,1)S(1)}, bf16[8,256,72]{1,2,0:T(8,128)(2,1)}, s32[]{:T(128)}, /*index=5*/s32[]{:T(128)}, s32[]{:T(128)}) while((s32[]{:T(128)}, bf16[8,256,576]{1,2,0:T(8,128)(2,1)S(1)}, bf16[8,256,288]{1,2,0:T(8,128)(2,1)S(1)}, ...), condition=%wide.region_1.2_spmd, body=%wide.region_0.1_spmd.sunk | while | flops 2 | bytes 4608145 | solution.py:61
  8.1 1.4 constant_dynamic-slice_fusion.2
  9.5 56.6 %all-gather.27.cloned.1.call-done = bf16[1,256,2304]{1,2,0:T(8,128)(2,1)} async-done(((bf16[1,256,72]{1,2,0:T(8,128)(2,1)}), bf16[1,256,2304]{1,2,0:T(8,128)(2,1)}) %all-gather.27.cloned.1.call-update) | async-done | bytes 1179664 | tf_op jit(solution)/shard_map/while/body/eval_jaxpr/all_gather | solution.py:56
  66.1 1.0 dynamic-slice_dynamic-update-slice_fusion.4
  67.1 0.9 dynamic-slice_dynamic-update-slice_fusion.5
  68.1 1.4 constant_dynamic-slice_fusion.2
  69.5 52.5 %all-gather.27.cloned.1.call-done = bf16[1,256,2304]{1,2,0:T(8,128)(2,1)} async-done(((bf16[1,256,72]{1,2,0:T(8,128)(2,1)}), bf16[1,256,2304]{1,2,0:T(8,128)(2,1)}) %all-gather.27.cloned.1.call-update) | async-done | bytes 1179664 | tf_op jit(solution)/shard_map/while/body/eval_jaxpr/all_gather | solution.py:56
  122.0 1.0 dynamic-slice_dynamic-update-slice_fusion.4
  124.0 1.4 constant_dynamic-slice_fusion.2
  125.4 52.5 %all-gather.27.cloned.1.call-done = bf16[1,256,2304]{1,2,0:T(8,128)(2,1)} async-done(((bf16[1,256,72]{1,2,0:T(8,128)(2,1)}), bf16[1,256,2304]{1,2,0:T(8,128)(2,1)}) %all-gather.27.cloned.1.call-update) | async-done | bytes 1179664 | tf_op jit(solution)/shard_map/while/body/eval_jaxpr/all_gather | solution.py:56
  177.9 1.0 dynamic-slice_dynamic-update-slice_fusion.4
  179.9 1.4 constant_dynamic-slice_fusion.2
  181.3 52.2 %all-gather.27.cloned.1.call-done = bf16[1,256,2304]{1,2,0:T(8,128)(2,1)} async-done(((bf16[1,256,72]{1,2,0:T(8,128)(2,1)}), bf16[1,256,2304]{1,2,0:T(8,128)(2,1)}) %all-gather.27.cloned.1.call-update) | async-done | bytes 1179664 | tf_op jit(solution)/shard_map/while/body/eval_jaxpr/all_gather | solution.py:56
  233.5 1.0 dynamic-slice_dynamic-update-slice_fusion.4
  235.5 1.4 constant_dynamic-slice_fusion.2
  236.9 52.2 %all-gather.27.cloned.1.call-done = bf16[1,256,2304]{1,2,0:T(8,128)(2,1)} async-done(((bf16[1,256,72]{1,2,0:T(8,128)(2,1)}), bf16[1,256,2304]{1,2,0:T(8,128)(2,1)}) %all-gather.27.cloned.1.call-update) | async-done | bytes 1179664 | tf_op jit(solution)/shard_map/while/body/eval_jaxpr/all_gather | solution.py:56
  289.1 1.0 dynamic-slice_dynamic-update-slice_fusion.4
  291.1 1.4 constant_dynamic-slice_fusion.2
  292.5 52.2 %all-gather.27.cloned.1.call-done = bf16[1,256,2304]{1,2,0:T(8,128)(2,1)} async-done(((bf16[1,256,72]{1,2,0:T(8,128)(2,1)}), bf16[1,256,2304]{1,2,0:T(8,128)(2,1)}) %all-gather.27.cloned.1.call-update) | async-done | bytes 1179664 | tf_op jit(solution)/shard_map/while/body/eval_jaxpr/all_gather | solution.py:56
  344.7 1.0 dynamic-slice_dynamic-update-slice_fusion.4
  346.7 1.4 constant_dynamic-slice_fusion.2
  348.1 52.5 %all-gather.27.cloned.1.call-done = bf16[1,256,2304]{1,2,0:T(8,128)(2,1)} async-done(((bf16[1,256,72]{1,2,0:T(8,128)(2,1)}), bf16[1,256,2304]{1,2,0:T(8,128)(2,1)}) %all-gather.27.cloned.1.call-update) | async-done | bytes 1179664 | tf_op jit(solution)/shard_map/while/body/eval_jaxpr/all_gather | solution.py:56
  400.6 1.0 dynamic-slice_dynamic-update-slice_fusion.4
  402.6 1.4 constant_dynamic-slice_fusion.2
  404.0 52.5 %all-gather.27.cloned.1.call-done = bf16[1,256,2304]{1,2,0:T(8,128)(2,1)} async-done(((bf16[1,256,72]{1,2,0:T(8,128)(2,1)}), bf16[1,256,2304]{1,2,0:T(8,128)(2,1)}) %all-gather.27.cloned.1.call-update) | async-done | bytes 1179664 | tf_op jit(solution)/shard_map/while/body/eval_jaxpr/all_gather | solution.py:56
  456.5 1.0 dynamic-slice_dynamic-update-slice_fusion.4
  458.5 3.7 fusion.83
  462.3 70.5 %reduce-scatter.2.cloned.1.call-done = f32[1,576,288]{1,2,0:T(8,128)} async-done(((f32[8,576,288]{1,2,0:T(8,128)}), f32[1,576,288]{1,2,0:T(8,128)}) %reduce-scatter.2.cloned.1.call-update) | async-done | bytes 663568 | tf_op jit(solution)/shard_map/reduce_scatter | solution.py:65
  532.8 2.1 fusion.48
  534.9 69.3 %psum.56 = f32[1]{0:T(128)} all-reduce(f32[1]{0:T(128)} %bitcast.4), channel_id=1, replica_groups=mesh['shard'=8,'tensor'=4,'section'=8] {'tensor','section'}, use_global_device_ids=true, to_apply=%region_4.5 | all-reduce | flops 1 | bytes 8 | tf_op jit(solution)/shard_map/psum | solution.py:71
  605.1 1.9 copy.32
  607.7 65.6 %all-gather.19.cloned.1.call-done = bf16[1,2304,288]{2,0,1:T(2,128)(2,1)} async-done(((bf16[1,576,288]{2,0,1:T(2,128)(2,1)}), bf16[1,2304,288]{2,0,1:T(2,128)(2,1)}) %all-gather.19.cloned.1.call-update) | async-done | bytes 1327120 | tf_op jit(solution)/shard_map/all_gather | solution.py:78
  673.3 8.4 copy.33
  681.7 29.2 %all-gather.17.cloned.1.call-done = bf16[1,576,2304]{1,2,0:T(8,128)(2,1)} async-done(((bf16[1,576,288]{1,2,0:T(8,128)(2,1)}), bf16[1,576,2304]{1,2,0:T(8,128)(2,1)}) %all-gather.17.cloned.1.call-update) | async-done | bytes 2654224 | tf_op jit(solution)/shard_map/all_gather | solution.py:79
  710.9 3.8 fusion.29
  715.5 41.7 %all-gather.25.cloned.1.call-done = bf16[4,576,288]{1,2,0:T(8,128)(2,1)} async-done(((bf16[1,576,288]{1,2,0:T(8,128)(2,1)}), bf16[4,576,288]{1,2,0:T(8,128)(2,1)}) %all-gather.25.cloned.1.call-update) | async-done | bytes 1327120 | tf_op jit(solution)/shard_map/all_gather | solution.py:80
  757.3 2.1 copy.34
  759.4 2.0 reshape.184
  761.4 24.7 %all-gather.15.cloned.1.call-done = bf16[1,576,2304]{1,2,0:T(8,128)(2,1)} async-done(((bf16[1,576,288]{1,2,0:T(8,128)(2,1)}), bf16[1,576,2304]{1,2,0:T(8,128)(2,1)}) %all-gather.15.cloned.1.call-update) | async-done | bytes 2654224 | tf_op jit(solution)/shard_map/all_gather | solution.py:81
  786.2 4.2 fusion.21
  790.6 19.7 %psum.60 = f32[8,8]{1,0:T(8,128)S(1)} all-reduce(f32[8,8]{1,0:T(8,128)S(1)} %fusion.84), channel_id=1, replica_groups=mesh['shard'=8,'tensor'=4,'section'=8] {'shard'}, use_global_device_ids=true, to_apply=%region_8.9 | all-reduce | flops 64 | bytes 512 | tf_op jit(solution)/shard_map/psum | solution.py:102
  812.3 15.1 %all-gather.4 = s32[8,1,256]{2,1,0:T(1,128)S(1)} all-gather(s32[1,1,256]{2,1,0:T(1,128)S(1)} %bitcast.152), channel_id=1, replica_groups=mesh['shard'=8,'tensor'=4,'section'=8] {'shard'}, dimensions={0}, use_global_device_ids=true | all-gather | bytes 9216 | tf_op jit(solution)/shard_map/all_gather | solution.py:124
  827.8 9.9 all-gather.21.cloned.1.call-done
  837.7 2.0 fusion.44
  839.7 2.0 fusion.43
  841.7 2.0 fusion.42
  843.7 2.0 fusion.41
  845.6 2.0 fusion.40
  847.6 56.9 %all-reduce.6 = bf16[5,256,288]{1,2,0:T(8,128)(2,1)S(1)} all-reduce(f32[5,256,288]{1,2,0:T(8,128)} %fusion.40), channel_id=1, replica_groups=mesh['shard'=8,'tensor'=4,'section'=8] {'tensor'}, use_global_device_ids=true, to_apply=%region_6.7 | all-reduce | flops 368640 | bytes 2211840 | tf_op jit(solution)/shard_map/psum | solution.py:97
  905.2 1.4 convolution_bitcast_fusion.2
  906.7 1.4 convolution_bitcast_fusion.1
  908.1 1.4 convolution_bitcast_fusion
  909.7 48.6 %all-reduce.7 = bf16[3,256,576]{1,2,0:T(8,128)(2,1)S(1)} all-reduce(f32[3,256,576]{1,2,0:T(8,128)S(1)} %pad_maximum_fusion), channel_id=1, replica_groups=mesh['shard'=8,'tensor'=4,'section'=8] {'section'}, use_global_device_ids=true, to_apply=%region_5.6 | all-reduce | flops 442368 | bytes 2654208 | tf_op jit(solution)/shard_map/psum | solution.py:90
  958.6 33.9 %all-reduce = (f32[8,576]{1,0:T(8,128)S(1)}, f32[2,72]{1,0:T(2,128)S(1)}, f32[2,72]{1,0:T(2,128)S(1)}) all-reduce(f32[8,576]{1,0:T(8,128)S(1)} %fusion.45, f32[2,72]{1,0:T(2,128)S(1)} %get-tuple-element.173, f32[2,72]{1,0:T(2,128)S(1)} %get-tuple-element.172), channel_id=1, replica_groups=mesh['shard'=8,'tensor'=4,'section'=8] {'shard'}, use_global_device_ids=true, to_apply=%region_10.11 | all-reduce | flops 4896 | bytes 39168 | tf_op jit(solution)/shard_map/psum | solution.py:131
  993.1 2.3 fusion.34
  996.6 2.5 copy.35
  999.2 17.1 %while.27 = (s32[]{:T(128)}, f32[4,512,288]{1,2,0:T(8,128)S(1)}, f32[4,512]{1,0:T(4,128)S(1)}, s32[4]{0:T(128)S(1)}, s32[]{:T(128)}, /*index=5*/s32[2048]{0:T(10...) while((s32[]{:T(128)}, f32[4,512,288]{1,2,0:T(8,128)S(1)}, f32[4,512]{1,0:T(4,128)S(1)}, ...), condition=%wide.region_17.18_spmd, body=%wide.region_15.17_spmd.sunk | while | flops 609222656 | bytes 1798293 | solution.py:145
  1000.3 2.5 fusion.99
  1004.5 2.5 fusion.99
  1008.8 2.5 fusion.99
  1013.1 2.5 fusion.99
  1017.2 1.7 broadcast_divide_fusion
  1018.9 67.6 %all-reduce.5.cloned.1.call-done = f32[4,576,288]{1,2,0:T(8,128)} async-done(((f32[4,576,288]{1,2,0:T(8,128)}), f32[4,576,288]{1,2,0:T(8,128)}) %all-reduce.5.cloned.1.call-update) | async-done | bytes 2654224 | tf_op jit(solution)/shard_map/psum | solution.py:131
  1086.5 3.7 broadcast_multiply_fusion
  (111 shorter events, 19.1 us)
Async XLA Ops:
  8.0 782.5 %copy-start = (bf16[8,256]{1,0:T(8,128)(2,1)S(1)}, bf16[8,256]{1,0:T(8,128)(2,1)}, u32[]{:S(2)}) copy-start(bf16[8,256]{1,0:T(8,128)(2,1)} %param.13) | copy-start | bytes 12292
  8.1 58.1 %all-gather.27.cloned.1.call-start = ((), (), s32[]{:S(2)}) async-start(), calls=%async_computation.9 | async-start | bytes 1216512 | tf_op jit(solution)/shard_map/while/body/eval_jaxpr/all_gather | solution.py:56
  68.0 54.0 %all-gather.27.cloned.1.call-start = ((), (), s32[]{:S(2)}) async-start(), calls=%async_computation.9 | async-start | bytes 1216512 | tf_op jit(solution)/shard_map/while/body/eval_jaxpr/all_gather | solution.py:56
  124.0 54.0 %all-gather.27.cloned.1.call-start = ((), (), s32[]{:S(2)}) async-start(), calls=%async_computation.9 | async-start | bytes 1216512 | tf_op jit(solution)/shard_map/while/body/eval_jaxpr/all_gather | solution.py:56
  179.9 53.7 %all-gather.27.cloned.1.call-start = ((), (), s32[]{:S(2)}) async-start(), calls=%async_computation.9 | async-start | bytes 1216512 | tf_op jit(solution)/shard_map/while/body/eval_jaxpr/all_gather | solution.py:56
  235.4 53.7 %all-gather.27.cloned.1.call-start = ((), (), s32[]{:S(2)}) async-start(), calls=%async_computation.9 | async-start | bytes 1216512 | tf_op jit(solution)/shard_map/while/body/eval_jaxpr/all_gather | solution.py:56
  291.0 53.7 %all-gather.27.cloned.1.call-start = ((), (), s32[]{:S(2)}) async-start(), calls=%async_computation.9 | async-start | bytes 1216512 | tf_op jit(solution)/shard_map/while/body/eval_jaxpr/all_gather | solution.py:56
  346.6 54.0 %all-gather.27.cloned.1.call-start = ((), (), s32[]{:S(2)}) async-start(), calls=%async_computation.9 | async-start | bytes 1216512 | tf_op jit(solution)/shard_map/while/body/eval_jaxpr/all_gather | solution.py:56
  402.5 54.0 %all-gather.27.cloned.1.call-start = ((), (), s32[]{:S(2)}) async-start(), calls=%async_computation.9 | async-start | bytes 1216512 | tf_op jit(solution)/shard_map/while/body/eval_jaxpr/all_gather | solution.py:56
  458.4 3.7 copy-start.5
  458.5 3.7 copy-start.7
  458.5 74.3 %reduce-scatter.2.cloned.1.call-start = ((), (), s32[]{:S(2)}) async-start(), calls=%async_computation.1 | async-start | bytes 6635520 | tf_op jit(solution)/shard_map/reduce_scatter | solution.py:65
  462.2 70.6 %copy-start.8 = (f32[1,576,288]{1,2,0:T(8,128)S(1)}, f32[1,576,288]{1,2,0:T(8,128)}, u32[]{:S(2)}) copy-start(f32[1,576,288]{1,2,0:T(8,128)} %param.16) | copy-start | bytes 1990660
  462.2 211.0 %all-gather.19.cloned.1.call-start = ((), (), s32[]{:S(2)}) async-start(), calls=%async_computation.4 | async-start | bytes 4423680 | tf_op jit(solution)/shard_map/all_gather | solution.py:78
  534.9 72.2 %copy-start.1 = (bf16[1,576,288]{1,2,0:T(8,128)(2,1)}, bf16[1,576,288]{1,2,0:T(8,128)(2,1)S(1)}, u32[]{:S(2)}) copy-start(bf16[1,576,288]{1,2,0:T(8,128)(2,1)S(1)} %get-tuple-element.206) | copy-start | bytes 995332
  605.1 76.6 %copy-start.3 = (bf16[1,576,288]{1,2,0:T(8,128)(2,1)}, bf16[1,576,288]{1,2,0:T(8,128)(2,1)S(1)}, u32[]{:S(2)}) copy-start(bf16[1,576,288]{1,2,0:T(8,128)(2,1)S(1)} %fusion.50) | copy-start | bytes 995332
  607.1 103.9 %all-gather.17.cloned.1.call-start = ((), (), s32[]{:S(2)}) async-start(), calls=%async_computation.3 | async-start | bytes 3317760 | tf_op jit(solution)/shard_map/all_gather | solution.py:79
  607.6 149.7 %all-gather.25.cloned.1.call-start = ((), (), s32[]{:S(2)}) async-start(), calls=%async_computation.8 | async-start | bytes 1843200 | tf_op jit(solution)/shard_map/all_gather | solution.py:80
  714.7 71.4 %all-gather.15.cloned.1.call-start = ((), (), s32[]{:S(2)}) async-start(), calls=%async_computation.2 | async-start | bytes 3317760 | tf_op jit(solution)/shard_map/all_gather | solution.py:81
  715.5 70.7 %copy-start.2 = (bf16[1,576,288]{1,2,0:T(8,128)(2,1)S(1)}, bf16[1,576,288]{1,2,0:T(8,128)(2,1)}, u32[]{:S(2)}) copy-start(bf16[1,576,288]{1,2,0:T(8,128)(2,1)} %copy-done.1) | copy-start | bytes 995332
  715.5 122.2 %all-gather.21.cloned.1.call-start = ((), (), s32[]{:S(2)}) async-start(), calls=%async_computation.5 | async-start | bytes 3317760 | tf_op jit(solution)/shard_map/all_gather | solution.py:83
  761.4 48.9 %copy-start.11 = (f32[8,8]{1,0:T(8,128)S(1)}, f32[8,8]{1,0:T(8,128)}, u32[]{:S(2)}) copy-start(f32[8,8]{1,0:T(8,128)} %param.17) | copy-start | bytes 772
  761.4 50.8 %copy-start.12 = (s32[256]{0:T(256)S(1)}, s32[256]{0:T(256)}, u32[]{:S(2)}) copy-start(s32[256]{0:T(256)} %param.14) | copy-start | bytes 3076
  761.4 65.9 %copy-start.9 = (bf16[2,256,72]{1,2,0:T(8,128)(2,1)S(1)}, bf16[2,256,72]{1,2,0:T(8,128)(2,1)}, u32[]{:S(2)}) copy-start(bf16[2,256,72]{1,2,0:T(8,128)(2,1)} %param.15) | copy-start | bytes 221188
  761.4 76.3 %copy-start.6 = (bf16[8,256,576]{1,2,0:T(8,128)(2,1)S(1)}, bf16[8,256,576]{1,2,0:T(8,128)(2,1)}, u32[]{:S(2)}) copy-start(bf16[8,256,576]{1,2,0:T(8,128)(2,1)} %copy-done.5) | copy-start | bytes 7077892
  790.4 206.2 %all-gather.23.cloned.1.call-start = ((), (), s32[]{:S(2)}) async-start(), calls=%async_computation.7 | async-start | bytes 1327104 | tf_op jit(solution)/shard_map/all_gather | solution.py:125
  905.2 181.3 %all-reduce.5.cloned.1.call-start = ((), (), s32[]{:S(2)}) async-start(), calls=%async_computation.6 | async-start | bytes 5898240 | tf_op jit(solution)/shard_map/psum | solution.py:131
  995.4 0.7 copy-start.13
  995.4 3.8 copy-start.4
  1016.5 0.7 copy-start.10
Sparse Core Ops, SparseCore 0:
  12.1 53.9 all-gather.26
  72.1 49.8 all-gather.26
  128.0 49.8 all-gather.26
  183.6 49.8 all-gather.26
  239.2 49.8 all-gather.26
  294.8 49.8 all-gather.26
  350.7 49.8 all-gather.26
  406.6 49.8 all-gather.26
Sparse Core Ops, SparseCore 1:
  462.3 70.4 reduce-scatter.1
  607.1 66.1 all-gather.18
  675.1 35.8 all-gather.16
  714.8 42.4 all-gather.24
  759.3 26.8 all-gather.14
  790.5 47.2 all-gather.20
  905.3 39.6 all-gather.22
  995.5 90.9 all-reduce.4
where the time goes:
time: 1100 us
  waiting for transfers between devices  734 us (67%)
  blocking collectives  243 us (22%)
  local copies, waits for them, and re-layouts  48.5 us (4%)
  matrix products  38.8 us (4%)
  between operations  17.2 us (2%)
  other arithmetic  12.2 us (1%)
    all_gather x8, waiting for transfers between devices, collect(): whole = lax.all_gather(piece, ('tensor', 'section'), axis=1, tiled=True)  423 us
    reduce_scatter x1, waiting for transfers between devices, per_device(): lax.psum_scatter(partial_value, 'shard', scatter_dimension=0, tiled=True)  70.5 us
    psum x1, blocking collectives, per_device(): trace = lax.psum(diag_part, ('tensor', 'section'))  69.3 us
    psum x1, waiting for transfers between devices, per_device(): attn_sum, router_total = lax.psum((attn_terms, router_term), 'shard')  67.6 us
    all_gather x1, waiting for transfers between devices, per_device(): first_cols = lax.all_gather(first_low, 'tensor', axis=1, tiled=True)  65.6 us
    psum x1, blocking collectives, per_device(): right = lax.psum(right_terms, 'tensor').astype(jnp.bfloat16)  56.9 us
    psum x1, blocking collectives, per_device(): left = lax.psum(left_terms, 'section').astype(jnp.bfloat16)  48.6 us
    all_gather x1, waiting for transfers between devices, per_device(): lax.all_gather(image.astype(jnp.bfloat16), 'tensor', axis=1, tiled=True)  41.7 us
  transfers between devices with their start and end apart: 16, of which 15 were waited for; matrix products, arithmetic and copies ran while one was open for 4% of the time, Pallas kernels for 0%

commit v1 on v0

--- a/solution.py
+++ b/solution.py
@@ -10,6 +10,11 @@
 factor_decay = 0.5
 damping = 0.01
 learning_rate = 0.05
+
+
+def by_each_axis(array, one, other):
+    partial = lax.psum(array, one)
+    return lax.psum(partial, other)
 
 
 def local_inverse(matrix):
@@ -68,7 +73,7 @@
     eye_block = (row_index == col_index).astype(jnp.float32)
     matrix = factor_decay * old_factors + (1.0 - factor_decay) * fresh + damping * eye_block
     diag_part = jnp.sum(matrix * eye_block, axis=(1, 2))
-    trace = lax.psum(diag_part, ("tensor", "section"))
+    trace = by_each_axis(diag_part, "tensor", "section")
     factor_scale = (D / (3.0 * trace))[:, None, None]
     matrix_low = lax.optimization_barrier(matrix.astype(jnp.bfloat16))
     first = 2.0 * factor_scale * eye_block - factor_scale * factor_scale * matrix_low.astype(

time: 1100 us -> 1050 us (0.955)
  blocking collectives: 243 us -> 197 us
    psum x1 -> x2, blocking collectives: 69.3 us -> 23.1 us  [the longest x1 12.4 us: by_each_axis(): partial = lax.psum(array, one)]
where the time goes in v1:
time: 1050 us
  waiting for transfers between devices  730 us (70%)
  blocking collectives  197 us (19%)
  local copies, waits for them, and re-layouts  49 us (5%)
  matrix products  38.8 us (4%)
  between operations  17.2 us (2%)
  other arithmetic  12.2 us (1%)
    all_gather x8, waiting for transfers between devices, collect(): whole = lax.all_gather(piece, ('tensor', 'section'), axis=1, tiled=True)  423 us
    reduce_scatter x1, waiting for transfers between devices, per_device(): lax.psum_scatter(partial_value, 'shard', scatter_dimension=0, tiled=True)  70.5 us
    psum x1, waiting for transfers between devices, per_device(): attn_sum, router_total = lax.psum((attn_terms, router_term), 'shard')  66.7 us
    all_gather x1, waiting for transfers between devices, per_device(): first_cols = lax.all_gather(first_low, 'tensor', axis=1, tiled=True)  62.6 us
    psum x1, blocking collectives, per_device(): right = lax.psum(right_terms, 'tensor').astype(jnp.bfloat16)  58.1 us
    psum x1, blocking collectives, per_device(): left = lax.psum(left_terms, 'section').astype(jnp.bfloat16)  48.5 us
    all_gather x1, waiting for transfers between devices, per_device(): lax.all_gather(image.astype(jnp.bfloat16), 'tensor', axis=1, tiled=True)  41.7 us
    psum x1, blocking collectives, per_device(): attn_sum, router_total = lax.psum((attn_terms, router_term), 'shard')  32.5 us
  transfers between devices with their start and end apart: 16, of which 15 were waited for; matrix products, arithmetic and copies ran while one was open for 4% of the time, Pallas kernels for 0%

profile of v1, /device:TPU:8, one launch (start us, length us, event | category | flops | bytes accessed | tf_op | source)
XLA Modules:
  0.0 1048.2 jit_solution(550658560823328849)
XLA Ops:
  8.0 450.4 %while.26 = (s32[]{:T(128)}, bf16[8,256,576]{1,2,0:T(8,128)(2,1)S(1)}, bf16[8,256,288]{1,2,0:T(8,128)(2,1)S(1)}, bf16[8,256,72]{1,2,0:T(8,128)(2,1)}, s32[]{:T(128)}, /*index=5*/s32[]{:T(128)}, s32[]{:T(128)}) while((s32[]{:T(128)}, bf16[8,256,576]{1,2,0:T(8,128)(2,1)S(1)}, bf16[8,256,288]{1,2,0:T(8,128)(2,1)S(1)}, ...), condition=%wide.region_1.2_spmd, body=%wide.region_0.1_spmd.sunk | while | flops 2 | bytes 4608145 | solution.py:66
  8.1 1.4 constant_dynamic-slice_fusion.2
  9.5 56.6 %all-gather.27.cloned.1.call-done = bf16[1,256,2304]{1,2,0:T(8,128)(2,1)} async-done(((bf16[1,256,72]{1,2,0:T(8,128)(2,1)}), bf16[1,256,2304]{1,2,0:T(8,128)(2,1)}) %all-gather.27.cloned.1.call-update) | async-done | bytes 1179664 | tf_op jit(solution)/shard_map/while/body/eval_jaxpr/all_gather | solution.py:61
  66.1 1.0 dynamic-slice_dynamic-update-slice_fusion.4
  68.1 1.4 constant_dynamic-slice_fusion.2
  69.5 52.5 %all-gather.27.cloned.1.call-done = bf16[1,256,2304]{1,2,0:T(8,128)(2,1)} async-done(((bf16[1,256,72]{1,2,0:T(8,128)(2,1)}), bf16[1,256,2304]{1,2,0:T(8,128)(2,1)}) %all-gather.27.cloned.1.call-update) | async-done | bytes 1179664 | tf_op jit(solution)/shard_map/while/body/eval_jaxpr/all_gather | solution.py:61
  122.0 1.0 dynamic-slice_dynamic-update-slice_fusion.4
  124.0 1.4 constant_dynamic-slice_fusion.2
  125.4 52.5 %all-gather.27.cloned.1.call-done = bf16[1,256,2304]{1,2,0:T(8,128)(2,1)} async-done(((bf16[1,256,72]{1,2,0:T(8,128)(2,1)}), bf16[1,256,2304]{1,2,0:T(8,128)(2,1)}) %all-gather.27.cloned.1.call-update) | async-done | bytes 1179664 | tf_op jit(solution)/shard_map/while/body/eval_jaxpr/all_gather | solution.py:61
  177.9 1.0 dynamic-slice_dynamic-update-slice_fusion.4
  179.9 1.4 constant_dynamic-slice_fusion.2
  181.3 52.2 %all-gather.27.cloned.1.call-done = bf16[1,256,2304]{1,2,0:T(8,128)(2,1)} async-done(((bf16[1,256,72]{1,2,0:T(8,128)(2,1)}), bf16[1,256,2304]{1,2,0:T(8,128)(2,1)}) %all-gather.27.cloned.1.call-update) | async-done | bytes 1179664 | tf_op jit(solution)/shard_map/while/body/eval_jaxpr/all_gather | solution.py:61
  233.5 1.0 dynamic-slice_dynamic-update-slice_fusion.4
  235.5 1.4 constant_dynamic-slice_fusion.2
  236.9 52.2 %all-gather.27.cloned.1.call-done = bf16[1,256,2304]{1,2,0:T(8,128)(2,1)} async-done(((bf16[1,256,72]{1,2,0:T(8,128)(2,1)}), bf16[1,256,2304]{1,2,0:T(8,128)(2,1)}) %all-gather.27.cloned.1.call-update) | async-done | bytes 1179664 | tf_op jit(solution)/shard_map/while/body/eval_jaxpr/all_gather | solution.py:61
  289.1 1.0 dynamic-slice_dynamic-update-slice_fusion.4
  291.1 1.4 constant_dynamic-slice_fusion.2
  292.5 52.2 %all-gather.27.cloned.1.call-done = bf16[1,256,2304]{1,2,0:T(8,128)(2,1)} async-done(((bf16[1,256,72]{1,2,0:T(8,128)(2,1)}), bf16[1,256,2304]{1,2,0:T(8,128)(2,1)}) %all-gather.27.cloned.1.call-update) | async-done | bytes 1179664 | tf_op jit(solution)/shard_map/while/body/eval_jaxpr/all_gather | solution.py:61
  344.7 1.0 dynamic-slice_dynamic-update-slice_fusion.4
  346.7 1.4 constant_dynamic-slice_fusion.2
  348.1 52.5 %all-gather.27.cloned.1.call-done = bf16[1,256,2304]{1,2,0:T(8,128)(2,1)} async-done(((bf16[1,256,72]{1,2,0:T(8,128)(2,1)}), bf16[1,256,2304]{1,2,0:T(8,128)(2,1)}) %all-gather.27.cloned.1.call-update) | async-done | bytes 1179664 | tf_op jit(solution)/shard_map/while/body/eval_jaxpr/all_gather | solution.py:61
  400.6 1.0 dynamic-slice_dynamic-update-slice_fusion.4
  402.6 1.4 constant_dynamic-slice_fusion.2
  404.0 52.5 %all-gather.27.cloned.1.call-done = bf16[1,256,2304]{1,2,0:T(8,128)(2,1)} async-done(((bf16[1,256,72]{1,2,0:T(8,128)(2,1)}), bf16[1,256,2304]{1,2,0:T(8,128)(2,1)}) %all-gather.27.cloned.1.call-update) | async-done | bytes 1179664 | tf_op jit(solution)/shard_map/while/body/eval_jaxpr/all_gather | solution.py:61
  456.5 1.0 dynamic-slice_dynamic-update-slice_fusion.4
  458.5 3.6 fusion.83
  462.3 70.5 %reduce-scatter.2.cloned.1.call-done = f32[1,576,288]{1,2,0:T(8,128)} async-done(((f32[8,576,288]{1,2,0:T(8,128)}), f32[1,576,288]{1,2,0:T(8,128)}) %reduce-scatter.2.cloned.1.call-update) | async-done | bytes 663568 | tf_op jit(solution)/shard_map/reduce_scatter | solution.py:70
  532.8 2.1 fusion.48
  534.9 12.4 %psum.63 = f32[1]{0:T(128)} all-reduce(f32[1]{0:T(128)} %bitcast.4), channel_id=1, replica_groups=mesh['shard'=8,'tensor'=4,'section'=8] {'tensor'}, use_global_device_ids=true, to_apply=%region_4.5 | all-reduce | flops 1 | bytes 8 | tf_op jit(solution)/shard_map/psum | solution.py:16
  547.3 10.6 %psum.64 = f32[1]{0:T(128)} all-reduce(f32[1]{0:T(128)} %psum.63), channel_id=1, replica_groups=mesh['shard'=8,'tensor'=4,'section'=8] {'section'}, use_global_device_ids=true, to_apply=%region_5.6 | all-reduce | flops 1 | bytes 8 | tf_op jit(solution)/shard_map/psum | solution.py:17
  558.8 1.9 copy.32
  561.4 62.6 %all-gather.19.cloned.1.call-done = bf16[1,2304,288]{2,0,1:T(2,128)(2,1)} async-done(((bf16[1,576,288]{2,0,1:T(2,128)(2,1)}), bf16[1,2304,288]{2,0,1:T(2,128)(2,1)}) %all-gather.19.cloned.1.call-update) | async-done | bytes 1327120 | tf_op jit(solution)/shard_map/all_gather | solution.py:83
  624.0 8.4 copy.33
  632.4 29.2 %all-gather.17.cloned.1.call-done = bf16[1,576,2304]{1,2,0:T(8,128)(2,1)} async-done(((bf16[1,576,288]{1,2,0:T(8,128)(2,1)}), bf16[1,576,2304]{1,2,0:T(8,128)(2,1)}) %all-gather.17.cloned.1.call-update) | async-done | bytes 2654224 | tf_op jit(solution)/shard_map/all_gather | solution.py:84
  661.7 3.8 fusion.29
  666.3 41.7 %all-gather.25.cloned.1.call-done = bf16[4,576,288]{1,2,0:T(8,128)(2,1)} async-done(((bf16[1,576,288]{1,2,0:T(8,128)(2,1)}), bf16[4,576,288]{1,2,0:T(8,128)(2,1)}) %all-gather.25.cloned.1.call-update) | async-done | bytes 1327120 | tf_op jit(solution)/shard_map/all_gather | solution.py:85
  708.0 2.1 copy.34
  710.2 2.0 reshape.184
  712.2 24.7 %all-gather.15.cloned.1.call-done = bf16[1,576,2304]{1,2,0:T(8,128)(2,1)} async-done(((bf16[1,576,288]{1,2,0:T(8,128)(2,1)}), bf16[1,576,2304]{1,2,0:T(8,128)(2,1)}) %all-gather.15.cloned.1.call-update) | async-done | bytes 2654224 | tf_op jit(solution)/shard_map/all_gather | solution.py:86
  736.9 4.2 fusion.21
  741.4 19.7 %psum.68 = f32[8,8]{1,0:T(8,128)S(1)} all-reduce(f32[8,8]{1,0:T(8,128)S(1)} %fusion.84), channel_id=1, replica_groups=mesh['shard'=8,'tensor'=4,'section'=8] {'shard'}, use_global_device_ids=true, to_apply=%region_9.10 | all-reduce | flops 64 | bytes 512 | tf_op jit(solution)/shard_map/psum | solution.py:107
  763.0 15.1 %all-gather.4 = s32[8,1,256]{2,1,0:T(1,128)S(1)} all-gather(s32[1,1,256]{2,1,0:T(1,128)S(1)} %bitcast.152), channel_id=1, replica_groups=mesh['shard'=8,'tensor'=4,'section'=8] {'shard'}, dimensions={0}, use_global_device_ids=true | all-gather | bytes 9216 | tf_op jit(solution)/shard_map/all_gather | solution.py:129
  778.5 10.0 all-gather.21.cloned.1.call-done
  788.5 2.0 fusion.44
  790.5 2.0 fusion.43
  792.5 2.0 fusion.42
  794.5 2.0 fusion.41
  796.4 2.0 fusion.40
  798.4 58.1 %all-reduce.6 = bf16[5,256,288]{1,2,0:T(8,128)(2,1)S(1)} all-reduce(f32[5,256,288]{1,2,0:T(8,128)} %fusion.40), channel_id=1, replica_groups=mesh['shard'=8,'tensor'=4,'section'=8] {'tensor'}, use_global_device_ids=true, to_apply=%region_7.8 | all-reduce | flops 368640 | bytes 2211840 | tf_op jit(solution)/shard_map/psum | solution.py:102
  857.3 1.4 convolution_bitcast_fusion.2
  858.7 1.4 convolution_bitcast_fusion.1
  860.1 1.4 convolution_bitcast_fusion
  861.7 48.5 %all-reduce.7 = bf16[3,256,576]{1,2,0:T(8,128)(2,1)S(1)} all-reduce(f32[3,256,576]{1,2,0:T(8,128)S(1)} %pad_maximum_fusion), channel_id=1, replica_groups=mesh['shard'=8,'tensor'=4,'section'=8] {'section'}, use_global_device_ids=true, to_apply=%region_6.7 | all-reduce | flops 442368 | bytes 2654208 | tf_op jit(solution)/shard_map/psum | solution.py:95
  910.6 32.5 %all-reduce = (f32[8,576]{1,0:T(8,128)S(1)}, f32[2,72]{1,0:T(2,128)S(1)}, f32[2,72]{1,0:T(2,128)S(1)}) all-reduce(f32[8,576]{1,0:T(8,128)S(1)} %fusion.45, f32[2,72]{1,0:T(2,128)S(1)} %get-tuple-element.173, f32[2,72]{1,0:T(2,128)S(1)} %get-tuple-element.172), channel_id=1, replica_groups=mesh['shard'=8,'tensor'=4,'section'=8] {'shard'}, use_global_device_ids=true, to_apply=%region_11.12 | all-reduce | flops 4896 | bytes 39168 | tf_op jit(solution)/shard_map/psum | solution.py:136
  943.7 2.3 fusion.34
  947.2 2.5 copy.35
  949.7 18.0 %while.27 = (s32[]{:T(128)}, f32[4,512,288]{1,2,0:T(8,128)S(1)}, f32[4,512]{1,0:T(4,128)S(1)}, s32[4]{0:T(128)S(1)}, s32[]{:T(128)}, /*index=5*/s32[2048]{0:T(10...) while((s32[]{:T(128)}, f32[4,512,288]{1,2,0:T(8,128)S(1)}, f32[4,512]{1,0:T(4,128)S(1)}, ...), condition=%wide.region_18.19_spmd, body=%wide.region_16.18_spmd.sunk | while | flops 609222656 | bytes 1798293 | solution.py:150
  951.1 2.5 fusion.99
  955.6 2.5 fusion.99
  960.1 2.5 fusion.99
  964.6 2.5 fusion.99
  968.7 1.7 broadcast_divide_fusion
  970.4 66.7 %all-reduce.5.cloned.1.call-done = f32[4,576,288]{1,2,0:T(8,128)} async-done(((f32[4,576,288]{1,2,0:T(8,128)}), f32[4,576,288]{1,2,0:T(8,128)}) %all-reduce.5.cloned.1.call-update) | async-done | bytes 2654224 | tf_op jit(solution)/shard_map/psum | solution.py:136
  1037.1 3.7 broadcast_multiply_fusion
  (112 shorter events, 20.5 us)
Async XLA Ops:
  8.0 733.2 %copy-start = (bf16[8,256]{1,0:T(8,128)(2,1)S(1)}, bf16[8,256]{1,0:T(8,128)(2,1)}, u32[]{:S(2)}) copy-start(bf16[8,256]{1,0:T(8,128)(2,1)} %param.13) | copy-start | bytes 12292
  8.1 58.1 %all-gather.27.cloned.1.call-start = ((), (), s32[]{:S(2)}) async-start(), calls=%async_computation.9 | async-start | bytes 1216512 | tf_op jit(solution)/shard_map/while/body/eval_jaxpr/all_gather | solution.py:61
  68.0 54.0 %all-gather.27.cloned.1.call-start = ((), (), s32[]{:S(2)}) async-start(), calls=%async_computation.9 | async-start | bytes 1216512 | tf_op jit(solution)/shard_map/while/body/eval_jaxpr/all_gather | solution.py:61
  124.0 54.0 %all-gather.27.cloned.1.call-start = ((), (), s32[]{:S(2)}) async-start(), calls=%async_computation.9 | async-start | bytes 1216512 | tf_op jit(solution)/shard_map/while/body/eval_jaxpr/all_gather | solution.py:61
  179.9 53.7 %all-gather.27.cloned.1.call-start = ((), (), s32[]{:S(2)}) async-start(), calls=%async_computation.9 | async-start | bytes 1216512 | tf_op jit(solution)/shard_map/while/body/eval_jaxpr/all_gather | solution.py:61
  235.4 53.7 %all-gather.27.cloned.1.call-start = ((), (), s32[]{:S(2)}) async-start(), calls=%async_computation.9 | async-start | bytes 1216512 | tf_op jit(solution)/shard_map/while/body/eval_jaxpr/all_gather | solution.py:61
  291.0 53.7 %all-gather.27.cloned.1.call-start = ((), (), s32[]{:S(2)}) async-start(), calls=%async_computation.9 | async-start | bytes 1216512 | tf_op jit(solution)/shard_map/while/body/eval_jaxpr/all_gather | solution.py:61
  346.6 54.0 %all-gather.27.cloned.1.call-start = ((), (), s32[]{:S(2)}) async-start(), calls=%async_computation.9 | async-start | bytes 1216512 | tf_op jit(solution)/shard_map/while/body/eval_jaxpr/all_gather | solution.py:61
  402.5 54.0 %all-gather.27.cloned.1.call-start = ((), (), s32[]{:S(2)}) async-start(), calls=%async_computation.9 | async-start | bytes 1216512 | tf_op jit(solution)/shard_map/while/body/eval_jaxpr/all_gather | solution.py:61
  458.4 3.7 copy-start.5
  458.5 3.7 copy-start.7
  458.5 74.3 %reduce-scatter.2.cloned.1.call-start = ((), (), s32[]{:S(2)}) async-start(), calls=%async_computation.1 | async-start | bytes 6635520 | tf_op jit(solution)/shard_map/reduce_scatter | solution.py:70
  462.2 70.6 %copy-start.8 = (f32[1,576,288]{1,2,0:T(8,128)S(1)}, f32[1,576,288]{1,2,0:T(8,128)}, u32[]{:S(2)}) copy-start(f32[1,576,288]{1,2,0:T(8,128)} %param.16) | copy-start | bytes 1990660
  462.2 161.8 %all-gather.19.cloned.1.call-start = ((), (), s32[]{:S(2)}) async-start(), calls=%async_computation.4 | async-start | bytes 4423680 | tf_op jit(solution)/shard_map/all_gather | solution.py:83
  534.9 26.0 %copy-start.1 = (bf16[1,576,288]{1,2,0:T(8,128)(2,1)}, bf16[1,576,288]{1,2,0:T(8,128)(2,1)S(1)}, u32[]{:S(2)}) copy-start(bf16[1,576,288]{1,2,0:T(8,128)(2,1)S(1)} %get-tuple-element.206) | copy-start | bytes 995332
  558.8 73.6 %copy-start.3 = (bf16[1,576,288]{1,2,0:T(8,128)(2,1)}, bf16[1,576,288]{1,2,0:T(8,128)(2,1)S(1)}, u32[]{:S(2)}) copy-start(bf16[1,576,288]{1,2,0:T(8,128)(2,1)S(1)} %fusion.50) | copy-start | bytes 995332
  560.8 100.9 %all-gather.17.cloned.1.call-start = ((), (), s32[]{:S(2)}) async-start(), calls=%async_computation.3 | async-start | bytes 3317760 | tf_op jit(solution)/shard_map/all_gather | solution.py:84
  561.4 146.7 %all-gather.25.cloned.1.call-start = ((), (), s32[]{:S(2)}) async-start(), calls=%async_computation.8 | async-start | bytes 1843200 | tf_op jit(solution)/shard_map/all_gather | solution.py:85
  665.5 71.4 %all-gather.15.cloned.1.call-start = ((), (), s32[]{:S(2)}) async-start(), calls=%async_computation.2 | async-start | bytes 3317760 | tf_op jit(solution)/shard_map/all_gather | solution.py:86
  666.2 70.7 %copy-start.2 = (bf16[1,576,288]{1,2,0:T(8,128)(2,1)S(1)}, bf16[1,576,288]{1,2,0:T(8,128)(2,1)}, u32[]{:S(2)}) copy-start(bf16[1,576,288]{1,2,0:T(8,128)(2,1)} %copy-done.1) | copy-start | bytes 995332
  666.2 122.3 %all-gather.21.cloned.1.call-start = ((), (), s32[]{:S(2)}) async-start(), calls=%async_computation.5 | async-start | bytes 3317760 | tf_op jit(solution)/shard_map/all_gather | solution.py:88
  712.2 48.9 %copy-start.11 = (f32[8,8]{1,0:T(8,128)S(1)}, f32[8,8]{1,0:T(8,128)}, u32[]{:S(2)}) copy-start(f32[8,8]{1,0:T(8,128)} %param.17) | copy-start | bytes 772
  712.2 50.8 %copy-start.12 = (s32[256]{0:T(256)S(1)}, s32[256]{0:T(256)}, u32[]{:S(2)}) copy-start(s32[256]{0:T(256)} %param.14) | copy-start | bytes 3076
  712.2 66.0 %copy-start.9 = (bf16[2,256,72]{1,2,0:T(8,128)(2,1)S(1)}, bf16[2,256,72]{1,2,0:T(8,128)(2,1)}, u32[]{:S(2)}) copy-start(bf16[2,256,72]{1,2,0:T(8,128)(2,1)} %param.15) | copy-start | bytes 221188
  712.2 76.3 %copy-start.6 = (bf16[8,256,576]{1,2,0:T(8,128)(2,1)S(1)}, bf16[8,256,576]{1,2,0:T(8,128)(2,1)}, u32[]{:S(2)}) copy-start(bf16[8,256,576]{1,2,0:T(8,128)(2,1)} %copy-done.5) | copy-start | bytes 7077892
  741.2 206.1 %all-gather.23.cloned.1.call-start = ((), (), s32[]{:S(2)}) async-start(), calls=%async_computation.7 | async-start | bytes 1327104 | tf_op jit(solution)/shard_map/all_gather | solution.py:130
  857.2 179.9 %all-reduce.5.cloned.1.call-start = ((), (), s32[]{:S(2)}) async-start(), calls=%async_computation.6 | async-start | bytes 5898240 | tf_op jit(solution)/shard_map/psum | solution.py:136
  946.0 0.7 copy-start.13
  946.0 3.8 copy-start.4
  968.0 0.7 copy-start.10
Sparse Core Ops, SparseCore 0:
  12.1 53.9 all-gather.26
  72.1 49.8 all-gather.26
  128.0 49.8 all-gather.26
  183.6 49.8 all-gather.26
  239.2 49.8 all-gather.26
  294.8 49.8 all-gather.26
  350.7 49.8 all-gather.26
  406.6 49.8 all-gather.26
Sparse Core Ops, SparseCore 1:
  462.3 70.4 reduce-scatter.1
  560.9 63.1 all-gather.18
  625.9 35.8 all-gather.16
  665.6 42.4 all-gather.24
  710.0 26.8 all-gather.14
  741.2 47.2 all-gather.20
  857.3 38.1 all-gather.22
  946.1 91.0 all-reduce.4
